TPU v7x, 256 devices: a whole 4x4x8 slice. The times are simulated.
256 devices in a mesh: wide: 64 (over y, z, core), narrow: 4 (over x).
Axes of the slice: x: 4, y: 4, z: 8, core: 2. Of those that a mesh axis runs over, the one named last changes fastest.
Arguments:
- embedding: float32 [131072, 128], P(('wide', 'narrow'))
- tile_blocks: bfloat16 [64, 4, 22, 512, 512], P('wide', 'narrow'), may hold values from -0.125 to 0.125
- tile_row: int32 [64, 4, 22], P('wide', 'narrow'), may hold values from 0 to 3
- tile_col: int32 [64, 4, 22], P('wide', 'narrow'), may hold values from 0 to 63
- counts: int32 [64, 4], P('wide', 'narrow'), may hold values from 1 to 22, as said below
Outputs:
- orthonormal: float32 [131072, 128], P(('wide', 'narrow'))
Inputs may be any that keep to these rules, and one draw needn't show every extreme that they name: Slots 0 to counts[w, n] - 1 of device (w, n) hold its tiles, the others are unused; some device has all 22 slots live.
All inputs are finite; a program needn't handle non-finite values.
Results may differ from a plain program's by a relative error of at most 0.0036.
Values may be sent and summed in bfloat16 or wider, within the bound.
No kernel may reach another device: no remote copies, remote signals or barrier semaphores. Data moves between devices by JAX's collectives and lax.ppermute only.
A program may use at most 64 MiB of HBM per device.

v0:
```python
import jax
import jax.numpy as jnp
from jax import lax
from jax.sharding import PartitionSpec as P


def apply_operator(values_bf, tile_local, row_local, col_local, live_count):
    tile_size = tile_local.shape[1]
    width = values_bf.shape[1]
    rows_dev = values_bf.shape[0]
    slab_count = lax.axis_size("narrow") * rows_dev // tile_size
    slot_count = tile_local.shape[0]
    gathered = lax.all_gather(values_bf, "wide", axis=0, tiled=True)
    blocks = gathered.reshape(-1, tile_size, width)
    picked = jnp.take(blocks, col_local, axis=0)
    products = jnp.einsum("sij,sjk->sik", tile_local, picked, preferred_element_type=jnp.float32)
    slot_ids = jnp.arange(slot_count, dtype=jnp.int32)
    slab_ids = jnp.arange(slab_count, dtype=jnp.int32)
    onehot = ((row_local[None, :] == slab_ids[:, None]) & (slot_ids[None, :] < live_count)).astype(
        jnp.float32
    )
    partial_value = jnp.einsum("rs,sik->rik", onehot, products, precision=lax.Precision.HIGHEST)
    partial_value = partial_value.reshape(slab_count * tile_size, width)
    slab_total = lax.psum(partial_value, "narrow")
    return lax.dynamic_slice_in_dim(slab_total, lax.axis_index("narrow") * rows_dev, rows_dev, 0)


def local(embedding, tile_blocks, tile_row, tile_col, counts):
    tile_local = tile_blocks[0, 0]
    row_local = tile_row[0, 0]
    col_local = tile_col[0, 0]
    live_count = counts[0, 0]
    emb_bf = embedding.astype(jnp.bfloat16)
    first_order = apply_operator(emb_bf, tile_local, row_local, col_local, live_count)
    first_bf = first_order.astype(jnp.bfloat16)
    second = (
        2.0 * apply_operator(first_bf, tile_local, row_local, col_local, live_count) - embedding
    )
    spectral = 1.2661 * embedding - 1.1303 * first_order + 0.2715 * second
    gram_part = lax.dot_general(
        spectral, spectral, (((0,), (0,)), ((), ())), precision=lax.Precision.HIGHEST
    )
    gram_matrix = lax.psum(gram_part, ("wide", "narrow"))
    lower_factor = jnp.linalg.cholesky(gram_matrix)
    solved = jax.scipy.linalg.solve_triangular(lower_factor, spectral.T, lower=True)
    node_total = embedding.shape[0] * lax.axis_size("wide") * lax.axis_size("narrow")
    return solved.T * jnp.sqrt(jnp.float32(node_total))


def solution(mesh):
    placed = (
        P(("wide", "narrow"), None),
        P("wide", "narrow", None, None, None),
        P("wide", "narrow", None),
        P("wide", "narrow", None),
        P("wide", "narrow"),
    )
    return jax.shard_map(
        local, mesh=mesh, in_specs=placed, out_specs=P(("wide", "narrow"), None), check_vma=False
    )
```

profile of v0, /device:TPU:1, one launch (start us, length us, event | category | flops | bytes accessed | tf_op | source)
XLA Modules:
  0.0 617.0 jit_solution(5770539556316250015)
XLA Ops:
  6.5 0.0 all-gather.3.cloned.1.call-start
  6.5 1.6 convert_element_type.8
  8.2 0.0 all-gather.3.cloned.1.call-update
  8.2 0.0 all-reduce.4.cloned.1.call-start
  8.9 0.7 compare_select_fusion
  9.6 0.7 compare_and_fusion
  10.2 87.1 %all-gather.3.cloned.1.call-done = bf16[32768,128]{1,0:T(8,128)(2,1)} async-done(((bf16[512,128]{1,0:T(8,128)(2,1)}), bf16[32768,128]{1,0:T(8,128)(2,1)}) %all-gather.3.cloned.1.call-update) | async-done | bytes 8388624 | tf_op jit(solution)/shard_map/all_gather | solution.py:13
  97.3 4.5 gather_fusion
  101.8 11.3 %fusion.2 = f32[22,128,512]{2,1,0:T(8,128)} fusion(bf16[1,1,22,512,512]{4,3,2,1,0:T(8,128)(2,1)} %param.8, bf16[22,512,128]{2,1,0:T(8,128)(2,1)S(1)} %gather_fusion, pred[22]{0:T(512)(128)(4,1)S(1)} %compare_and_fusion), kind=kOutput, calls=%fused_computation.4 | convolution fusion | flops 1477836800 | bytes 20185110 | tf_op jit(solution)/shard_map/sij,sjk->sik/dot_general | solution.py:16
  113.1 0.0 copy-start.1
  113.1 6.5 %copy.12 = f32[22,128,512]{1,0,2:T(8,128)} copy(f32[22,128,512]{2,1,0:T(8,128)} %fusion.2) | data formatting | bytes 11534336 | tf_op jit(solution)/shard_map/sij,sjk->sik/dot_general | solution.py:16
  119.6 0.0 copy-done.1
  119.6 5.0 fusion.6
  124.6 1.0 copy.8
  125.6 0.0 all-reduce.4.cloned.1.call-update
  125.6 0.0 all-gather.5.cloned.1.call-start
  125.7 45.8 %all-reduce.4.cloned.1.call-done = f32[2048,128]{1,0:T(8,128)} async-done(((f32[2048,128]{1,0:T(8,128)}), f32[2048,128]{1,0:T(8,128)}) %all-reduce.4.cloned.1.call-update) | async-done | bytes 1048592 | tf_op jit(solution)/shard_map/psum | solution.py:24
  171.5 1.6 dynamic-slice_convert_fusion
  173.2 0.0 all-gather.5.cloned.1.call-update
  173.2 0.2 all-reduce.6.cloned.1.call-start
  173.4 87.1 %all-gather.5.cloned.1.call-done = bf16[32768,128]{1,0:T(8,128)(2,1)} async-done(((bf16[512,128]{1,0:T(8,128)(2,1)}), bf16[32768,128]{1,0:T(8,128)(2,1)}) %all-gather.5.cloned.1.call-update) | async-done | bytes 8388624 | tf_op jit(solution)/shard_map/all_gather | solution.py:13
  260.5 4.5 gather_fusion.1
  265.0 11.3 %fusion = f32[22,128,512]{2,1,0:T(8,128)} fusion(bf16[1,1,22,512,512]{4,3,2,1,0:T(8,128)(2,1)} %param.8, bf16[22,512,128]{2,1,0:T(8,128)(2,1)S(1)} %gather_fusion.1, pred[22]{0:T(512)(128)(4,1)S(1)} %compare_and_fusion), kind=kOutput, calls=%fused_computation.2 | convolution fusion | flops 1477836800 | bytes 20185110 | tf_op jit(solution)/shard_map/sij,sjk->sik/dot_general | solution.py:16
  276.3 6.4 %copy.13 = f32[22,128,512]{1,0,2:T(8,128)} copy(f32[22,128,512]{2,1,0:T(8,128)} %fusion) | data formatting | bytes 11534336 | tf_op jit(solution)/shard_map/sij,sjk->sik/dot_general | solution.py:16
  282.7 0.0 copy-start
  282.7 5.1 fusion.4
  287.8 1.1 copy.9
  288.9 0.0 all-reduce.6.cloned.1.call-update
  288.9 0.3 all-reduce.8.cloned.1.call-start
  289.2 45.6 %all-reduce.6.cloned.1.call-done = f32[2048,128]{1,0:T(8,128)} async-done(((f32[2048,128]{1,0:T(8,128)}), f32[2048,128]{1,0:T(8,128)}) %all-reduce.6.cloned.1.call-update) | async-done | bytes 1048592 | tf_op jit(solution)/shard_map/psum | solution.py:24
  334.8 0.0 copy-done
  334.8 1.1 multiply_add_fusion
  335.9 1.2 fusion.23
  337.1 0.0 all-reduce.8.cloned.1.call-update
  337.1 247.6 %all-reduce.8.cloned.1.call-done = f32[128,128]{0,1:T(8,128)} async-done(((f32[128,128]{0,1:T(8,128)}), f32[128,128]{0,1:T(8,128)}) %all-reduce.8.cloned.1.call-update) | async-done | bytes 65552 | tf_op jit(solution)/shard_map/psum | solution.py:43
  584.7 0.9 copy.11
  585.6 0.9 fusion.16
  586.5 11.7 %cholesky.16 = f32[128,128]{1,0:T(8,128)S(1)} custom-call(f32[128,128]{1,0:T(8,128)S(1)} %fusion.16), custom_call_target="Cholesky" | custom-call | tf_op jit(solution)/shard_map/jit(cholesky)/cholesky | solution.py:44
  598.2 0.6 compare_reduce_fusion
  598.9 0.7 fusion.14
  599.5 9.8 %custom-call.7 = f32[1,128,128]{1,2,0:T(8,128)S(1)} custom-call(f32[1,128,128]{2,1,0:T(8,128)S(1)} %fusion.14), custom_call_target="InvertDiagBlocksLowerTriangular" | custom-call | tf_op jit(solution)/shard_map/jit(_solve_triangular)/triangular_solve | solution.py:45
  609.4 1.1 convolution_multiply_fusion
  (3 shorter events, 0.1 us)
Async XLA Ops:
  6.5 90.8 %all-gather.3.cloned.1.call-start = ((), (), s32[]{:S(2)}) async-start(), calls=%async_computation | async-start | bytes 8519680 | tf_op jit(solution)/shard_map/all_gather | solution.py:13
  8.2 163.4 %all-reduce.4.cloned.1.call-start = ((), (), s32[]{:S(2)}) async-start(), calls=%async_computation.1 | async-start | bytes 2097152 | tf_op jit(solution)/shard_map/psum | solution.py:24
  113.1 6.5 %copy-start.1 = (s32[1,1,22]{2,1,0:T(1,128)S(1)}, s32[1,1,22]{2,1,0:T(1,128)}, u32[]{:S(2)}) copy-start(s32[1,1,22]{2,1,0:T(1,128)} %param.9) | copy-start | bytes 268
  125.6 134.9 %all-gather.5.cloned.1.call-start = ((), (), s32[]{:S(2)}) async-start(), calls=%async_computation.2 | async-start | bytes 8519680 | tf_op jit(solution)/shard_map/all_gather | solution.py:13
  173.2 161.6 %all-reduce.6.cloned.1.call-start = ((), (), s32[]{:S(2)}) async-start(), calls=%async_computation.3 | async-start | bytes 2097152 | tf_op jit(solution)/shard_map/psum | solution.py:24
  282.7 52.1 %copy-start = (f32[512,128]{1,0:T(8,128)S(1)}, f32[512,128]{1,0:T(8,128)}, u32[]{:S(2)}) copy-start(f32[512,128]{1,0:T(8,128)} %param.7) | copy-start | bytes 786436
  288.9 295.8 %all-reduce.8.cloned.1.call-start = ((), (), s32[]{:S(2)}) async-start(), calls=%async_computation.4 | async-start | bytes 131072 | tf_op jit(solution)/shard_map/psum | solution.py:43
Sparse Core Ops, SparseCore 0:
  10.1 87.1 all-gather.2
  125.8 45.7 all-reduce.3
  174.3 86.1 all-gather.4
  289.0 45.7 all-reduce.5
  340.1 244.5 all-reduce.7
where the time goes:
time: 618 us; the launch traced here: 617 us
  waiting for transfers between devices  513 us (83%)
  matrix products  34.9 us (6%)
  other arithmetic  27.8 us (4%)
  local copies, waits for them, and re-layouts  26.5 us (4%)
  between operations  13.9 us (2%)
    psum x1, waiting for transfers between devices, local(): gram_matrix = lax.psum(gram_part, ('wide', 'narrow'))  248 us
    all_gather x2, waiting for transfers between devices, apply_operator(): gathered = lax.all_gather(values_bf, 'wide', axis=0, tiled=True)  174 us
    psum x2, waiting for transfers between devices, apply_operator(): slab_total = lax.psum(partial_value, 'narrow')  91.4 us
    dot_general x2, matrix products, apply_operator(): jnp.einsum('sij,sjk->sik', tile_local, picked, preferred_element_type=jnp...  22.5 us
    dot_general x2, local copies, waits for them, and re-layouts, apply_operator(): jnp.einsum('sij,sjk->sik', tile_local, picked, preferred_element_type=jnp...  12.9 us
    another operation x3, other arithmetic, local(): lower_factor = jnp.linalg.cholesky(gram_matrix)  12.4 us
  transfers between devices with their start and end apart: 5, of which 5 were waited for; matrix products, arithmetic and copies ran while one was open for 0% of the time, Pallas kernels for 0%

commit v1 on v0

--- a/solution.py
+++ b/solution.py
@@ -2,6 +2,7 @@
 import jax.numpy as jnp
 from jax import lax
 from jax.sharding import PartitionSpec as P
+from jax.lax import psum
 
 
 def apply_operator(values_bf, tile_local, row_local, col_local, live_count):
@@ -40,7 +41,7 @@
     gram_part = lax.dot_general(
         spectral, spectral, (((0,), (0,)), ((), ())), precision=lax.Precision.HIGHEST
     )
-    gram_matrix = lax.psum(gram_part, ("wide", "narrow"))
+    gram_matrix = psum(psum(gram_part, "narrow"), "wide")
     lower_factor = jnp.linalg.cholesky(gram_matrix)
     solved = jax.scipy.linalg.solve_triangular(lower_factor, spectral.T, lower=True)
     node_total = embedding.shape[0] * lax.axis_size("wide") * lax.axis_size("narrow")

time: 618 us -> 594 us (0.961)
  waiting for transfers between devices: 513 us -> 490 us
    psum x1 -> x2, waiting for transfers between devices: 248 us -> 224 us  [local(): gram_matrix = psum(psum(gram_part, 'narrow'), 'wide')]
  transfers between devices with their start and end apart: 5 -> 6, of which waited for: 5 -> 6; matrix products, arithmetic and copies ran while one was open for 0% -> 0% of each run, Pallas kernels for 0% -> 0%
where the time goes in v1:
time: 594 us
  waiting for transfers between devices  490 us (82%)
  matrix products  34.9 us (6%)
  other arithmetic  27.8 us (5%)
  local copies, waits for them, and re-layouts  26.5 us (4%)
  between operations  14.2 us (2%)
    psum x2, waiting for transfers between devices, local(): gram_matrix = psum(psum(gram_part, 'narrow'), 'wide')  224 us
    all_gather x2, waiting for transfers between devices, apply_operator(): gathered = lax.all_gather(values_bf, 'wide', axis=0, tiled=True)  174 us
    psum x2, waiting for transfers between devices, apply_operator(): slab_total = lax.psum(partial_value, 'narrow')  91.7 us
    dot_general x2, matrix products, apply_operator(): jnp.einsum('sij,sjk->sik', tile_local, picked, preferred_element_type=jnp...  22.5 us
    dot_general x2, local copies, waits for them, and re-layouts, apply_operator(): jnp.einsum('sij,sjk->sik', tile_local, picked, preferred_element_type=jnp...  12.9 us
    another operation x3, other arithmetic, local(): lower_factor = jnp.linalg.cholesky(gram_matrix)  12.4 us
  transfers between devices with their start and end apart: 6, of which 6 were waited for; matrix products, arithmetic and copies ran while one was open for 0% of the time, Pallas kernels for 0%

profile of v1, /device:TPU:1, one launch (start us, length us, event | category | flops | bytes accessed | tf_op | source)
XLA Modules:
  0.0 593.8 jit_solution(17378647761954434075)
XLA Ops:
  6.5 0.0 all-gather.3.cloned.1.call-start
  6.5 1.6 convert_element_type.8
  8.2 0.0 all-gather.3.cloned.1.call-update
  8.2 0.0 all-reduce.5.cloned.1.call-start
  8.9 0.7 compare_select_fusion
  9.6 0.7 compare_and_fusion
  10.2 87.1 %all-gather.3.cloned.1.call-done = bf16[32768,128]{1,0:T(8,128)(2,1)} async-done(((bf16[512,128]{1,0:T(8,128)(2,1)}), bf16[32768,128]{1,0:T(8,128)(2,1)}) %all-gather.3.cloned.1.call-update) | async-done | bytes 8388624 | tf_op jit(solution)/shard_map/all_gather | solution.py:14
  97.3 4.5 gather_fusion
  101.8 11.3 %fusion.2 = f32[22,128,512]{2,1,0:T(8,128)} fusion(bf16[1,1,22,512,512]{4,3,2,1,0:T(8,128)(2,1)} %param.8, bf16[22,512,128]{2,1,0:T(8,128)(2,1)S(1)} %gather_fusion, pred[22]{0:T(512)(128)(4,1)S(1)} %compare_and_fusion), kind=kOutput, calls=%fused_computation.4 | convolution fusion | flops 1477836800 | bytes 20185110 | tf_op jit(solution)/shard_map/sij,sjk->sik/dot_general | solution.py:17
  113.1 0.0 copy-start.1
  113.1 6.5 %copy.12 = f32[22,128,512]{1,0,2:T(8,128)} copy(f32[22,128,512]{2,1,0:T(8,128)} %fusion.2) | data formatting | bytes 11534336 | tf_op jit(solution)/shard_map/sij,sjk->sik/dot_general | solution.py:17
  119.6 0.0 copy-done.1
  119.6 5.0 fusion.6
  124.6 1.0 copy.8
  125.6 0.0 all-reduce.5.cloned.1.call-update
  125.6 0.0 all-gather.5.cloned.1.call-start
  125.7 45.8 %all-reduce.5.cloned.1.call-done = f32[2048,128]{1,0:T(8,128)} async-done(((f32[2048,128]{1,0:T(8,128)}), f32[2048,128]{1,0:T(8,128)}) %all-reduce.5.cloned.1.call-update) | async-done | bytes 1048592 | tf_op jit(solution)/shard_map/psum | solution.py:25
  171.5 1.6 dynamic-slice_convert_fusion
  173.2 0.0 all-gather.5.cloned.1.call-update
  173.2 0.2 all-reduce.7.cloned.1.call-start
  173.4 87.1 %all-gather.5.cloned.1.call-done = bf16[32768,128]{1,0:T(8,128)(2,1)} async-done(((bf16[512,128]{1,0:T(8,128)(2,1)}), bf16[32768,128]{1,0:T(8,128)(2,1)}) %all-gather.5.cloned.1.call-update) | async-done | bytes 8388624 | tf_op jit(solution)/shard_map/all_gather | solution.py:14
  260.5 4.5 gather_fusion.1
  265.0 11.3 %fusion = f32[22,128,512]{2,1,0:T(8,128)} fusion(bf16[1,1,22,512,512]{4,3,2,1,0:T(8,128)(2,1)} %param.8, bf16[22,512,128]{2,1,0:T(8,128)(2,1)S(1)} %gather_fusion.1, pred[22]{0:T(512)(128)(4,1)S(1)} %compare_and_fusion), kind=kOutput, calls=%fused_computation.2 | convolution fusion | flops 1477836800 | bytes 20185110 | tf_op jit(solution)/shard_map/sij,sjk->sik/dot_general | solution.py:17
  276.3 6.4 %copy.13 = f32[22,128,512]{1,0,2:T(8,128)} copy(f32[22,128,512]{2,1,0:T(8,128)} %fusion) | data formatting | bytes 11534336 | tf_op jit(solution)/shard_map/sij,sjk->sik/dot_general | solution.py:17
  282.7 0.0 copy-start
  282.7 5.1 fusion.4
  287.8 1.1 copy.9
  288.9 0.0 all-reduce.7.cloned.1.call-update
  288.9 0.0 all-reduce.9.cloned.1.call-start
  289.0 45.8 %all-reduce.7.cloned.1.call-done = f32[2048,128]{1,0:T(8,128)} async-done(((f32[2048,128]{1,0:T(8,128)}), f32[2048,128]{1,0:T(8,128)}) %all-reduce.7.cloned.1.call-update) | async-done | bytes 1048592 | tf_op jit(solution)/shard_map/psum | solution.py:25
  334.8 0.0 copy-done
  334.8 1.1 multiply_add_fusion
  335.9 1.2 fusion.23
  337.1 0.0 all-reduce.9.cloned.1.call-update
  337.1 0.3 all-reduce.11.cloned.1.call-start
  337.4 46.9 %all-reduce.9.cloned.1.call-done = f32[128,128]{0,1:T(8,128)} async-done(((f32[128,128]{0,1:T(8,128)}), f32[128,128]{0,1:T(8,128)}) %all-reduce.9.cloned.1.call-update) | async-done | bytes 65552 | tf_op jit(solution)/shard_map/psum | solution.py:44
  384.3 0.0 all-reduce.11.cloned.1.call-update
  384.3 176.9 %all-reduce.11.cloned.1.call-done = f32[128,128]{0,1:T(8,128)} async-done(((f32[128,128]{0,1:T(8,128)}), f32[128,128]{0,1:T(8,128)}) %all-reduce.11.cloned.1.call-update) | async-done | bytes 65552 | tf_op jit(solution)/shard_map/psum | solution.py:44
  561.2 0.9 copy.11
  562.1 0.9 fusion.16
  563.0 11.7 %cholesky.16 = f32[128,128]{1,0:T(8,128)S(1)} custom-call(f32[128,128]{1,0:T(8,128)S(1)} %fusion.16), custom_call_target="Cholesky" | custom-call | tf_op jit(solution)/shard_map/jit(cholesky)/cholesky | solution.py:45
  574.8 0.6 compare_reduce_fusion
  575.4 0.7 fusion.14
  576.1 9.8 %custom-call.7 = f32[1,128,128]{1,2,0:T(8,128)S(1)} custom-call(f32[1,128,128]{2,1,0:T(8,128)S(1)} %fusion.14), custom_call_target="InvertDiagBlocksLowerTriangular" | custom-call | tf_op jit(solution)/shard_map/jit(_solve_triangular)/triangular_solve | solution.py:46
  585.9 1.1 convolution_multiply_fusion
  (3 shorter events, 0.1 us)
Async XLA Ops:
  6.5 90.8 %all-gather.3.cloned.1.call-start = ((), (), s32[]{:S(2)}) async-start(), calls=%async_computation | async-start | bytes 8519680 | tf_op jit(solution)/shard_map/all_gather | solution.py:14
  8.2 163.4 %all-reduce.5.cloned.1.call-start = ((), (), s32[]{:S(2)}) async-start(), calls=%async_computation.1 | async-start | bytes 2097152 | tf_op jit(solution)/shard_map/psum | solution.py:25
  113.1 6.5 %copy-start.1 = (s32[1,1,22]{2,1,0:T(1,128)S(1)}, s32[1,1,22]{2,1,0:T(1,128)}, u32[]{:S(2)}) copy-start(s32[1,1,22]{2,1,0:T(1,128)} %param.9) | copy-start | bytes 268
  125.6 134.9 %all-gather.5.cloned.1.call-start = ((), (), s32[]{:S(2)}) async-start(), calls=%async_computation.2 | async-start | bytes 8519680 | tf_op jit(solution)/shard_map/all_gather | solution.py:14
  173.2 161.6 %all-reduce.7.cloned.1.call-start = ((), (), s32[]{:S(2)}) async-start(), calls=%async_computation.3 | async-start | bytes 2097152 | tf_op jit(solution)/shard_map/psum | solution.py:25
  282.7 52.1 %copy-start = (f32[512,128]{1,0:T(8,128)S(1)}, f32[512,128]{1,0:T(8,128)}, u32[]{:S(2)}) copy-start(f32[512,128]{1,0:T(8,128)} %param.7) | copy-start | bytes 786436
  288.9 95.4 %all-reduce.9.cloned.1.call-start = ((), (), s32[]{:S(2)}) async-start(), calls=%async_computation.4 | async-start | bytes 131072 | tf_op jit(solution)/shard_map/psum | solution.py:44
  337.1 224.1 %all-reduce.11.cloned.1.call-start = ((), (), s32[]{:S(2)}) async-start(), calls=%async_computation.5 | async-start | bytes 131072 | tf_op jit(solution)/shard_map/psum | solution.py:44
Sparse Core Ops, SparseCore 0:
  10.1 87.1 all-gather.2
  125.8 45.7 all-reduce.4
  174.3 86.1 all-gather.4
  289.0 45.7 all-reduce.6
  337.3 46.9 all-reduce.8
  387.6 173.5 all-reduce.10
